TPU v7x, 512 devices: a whole 4x8x8 slice. The times are simulated.
512 devices in a mesh: track: 64 (over z, x, core), ses: 8 (over y).
Axes of the slice: x: 4, y: 8, z: 8, core: 2. Of those that a mesh axis runs over, the one named last changes fastest.
Arguments:
- jacobians: float32 [2, 9, 8, 131072], P(None, None, None, ('track', 'ses')), may hold values from -6 to 6
- direction: float32 [6, 2097152], P(None, ('track', 'ses')), may hold values from -50 to 50
- residual: float32 [6, 2097152], P(None, ('track', 'ses')), may hold values from -50 to 50
- solution: float32 [6, 2097152], P(None, ('track', 'ses')), may hold values from -6 to 6
- cam_damping: float32 [6, 2097152], P(None, ('track', 'ses')), may hold values from 0.5 to 4
- precond: float32 [6, 6, 2097152], P(None, None, ('track', 'ses')), may hold values from -0.15 to 2, as said below
- land_damping: float32 [131072], P(('track', 'ses')), may hold values from 0.5 to 4
- obs_slot: int32 [8, 131072], P(None, ('track', 'ses')), may hold values from 0 to 8191, as said below
- obs_mask: int32 [8, 131072], P(None, ('track', 'ses')), may hold values from 0 to 1, as said below
- serve_rows: int32 [512, 8192], P(('track', 'ses')), may hold values from 0 to 4095, as said below
Outputs:
- solution_new: float32 [6, 2097152], P(None, ('track', 'ses'))
- residual_new: float32 [6, 2097152], P(None, ('track', 'ses'))
- direction_new: float32 [6, 2097152], P(None, ('track', 'ses'))
Inputs may be any that keep to these rules, and one draw needn't show every extreme that they name: `obs_slot`: each slot names one keyframe that device s // 16 serves to the observing device; most slots name an owner in the observing device's own session block, the rest name owners anywhere. `serve_rows`: each row block of 16 entries lists distinct local keyframe rows of the owner. `obs_mask`: A track's live observation slots come first; every track has 2 to 8. `precond`: Symmetric, with a dominant positive diagonal.
All inputs are finite; a program needn't handle non-finite values.
Results may differ from a plain program's by a relative error of at most 0.0003.
Values sent between devices are 32-bit elements; how exact they have to be, the bound alone decides.
A program may use at most 64 MiB of HBM per device.

v0:
```python
import jax
import jax.numpy as jnp
from jax import lax
from jax.sharding import PartitionSpec as P


def invert_three(matrix):
    cofactor = [
        [
            matrix[(i + 1) % 3, (j + 1) % 3] * matrix[(i + 2) % 3, (j + 2) % 3]
            - matrix[(i + 1) % 3, (j + 2) % 3] * matrix[(i + 2) % 3, (j + 1) % 3]
            for j in range(3)
        ]
        for i in range(3)
    ]
    determinant = (
        matrix[0, 0] * cofactor[0][0]
        + matrix[0, 1] * cofactor[0][1]
        + matrix[0, 2] * cofactor[0][2]
    )
    adjugate = jnp.stack([jnp.stack([cofactor[j][i] for j in range(3)]) for i in range(3)])
    return adjugate / determinant[None, None]


def track_terms(jacobian, camera_rows, live_mask, land_damp):
    cam_jac = jacobian[:, 0:6]
    land_jac = jacobian[:, 6:9]
    projected = jnp.sum(cam_jac * camera_rows[None], axis=1)
    weighted = land_jac * live_mask[None, None]
    normal_mat = jnp.sum(weighted[:, :, None] * land_jac[:, None, :], axis=(0, 3))
    identity_mat = (jnp.arange(3)[:, None] == jnp.arange(3)[None, :]).astype(jnp.float32)
    normal_mat = normal_mat + identity_mat[:, :, None] * land_damp[None, None]
    inverse = invert_three(normal_mat)
    landmark_rhs = jnp.sum(weighted * projected[:, None], axis=(0, 2))
    landmark_step = jnp.sum(inverse * landmark_rhs[None], axis=1)
    back_proj = jnp.sum(land_jac * landmark_step[None, :, None], axis=1)
    obs_res = live_mask[None] * (projected - back_proj)
    return jnp.sum(cam_jac * obs_res[:, None], axis=0)


def apply_precond(precond, vector):
    return jnp.sum(precond * vector[None], axis=1)


def on_device(
    jacobians,
    direction,
    residual,
    solution,
    cam_damping,
    precond,
    land_damping,
    obs_slot,
    obs_mask,
    serve_rows,
):
    track_count = lax.axis_size("track")
    ses_count = lax.axis_size("ses")
    served = serve_rows.reshape(-1)
    capacity = served.shape[0] // (track_count * ses_count)
    outgoing = direction[:, served].reshape(6, track_count, ses_count, capacity)
    incoming = lax.all_to_all(
        lax.all_to_all(outgoing, "track", split_axis=1, concat_axis=1, tiled=True),
        "ses",
        split_axis=2,
        concat_axis=2,
        tiled=True,
    )
    incoming = incoming.reshape(6, -1)
    camera_rows = incoming[:, obs_slot]
    live_mask = obs_mask.astype(jnp.float32)
    gradient = track_terms(jacobians, camera_rows, live_mask, land_damping)
    slot_sums = (
        jnp.zeros(incoming.shape, jnp.float32)
        .at[:, obs_slot.reshape(-1)]
        .add(gradient.reshape(6, -1))
    )
    slot_sums = slot_sums.reshape(6, track_count, ses_count, capacity)
    arrived = lax.all_to_all(
        lax.all_to_all(slot_sums, "track", split_axis=1, concat_axis=1, tiled=True),
        "ses",
        split_axis=2,
        concat_axis=2,
        tiled=True,
    )
    summed = jnp.zeros(direction.shape, jnp.float32).at[:, served].add(arrived.reshape(6, -1))
    schur_image = cam_damping * direction + summed
    precond_old = apply_precond(precond, residual)
    old_norm = lax.psum(jnp.sum(residual * precond_old), ("track", "ses"))
    curvature = lax.psum(jnp.sum(direction * schur_image), ("track", "ses"))
    step_size = old_norm / curvature
    solution_new = solution + step_size * direction
    residual_new = residual - step_size * schur_image
    precond_res = apply_precond(precond, residual_new)
    new_norm = lax.psum(jnp.sum(residual_new * precond_res), ("track", "ses"))
    direction_new = precond_res + new_norm / old_norm * direction
    return (solution_new, residual_new, direction_new)


def solution(mesh):
    return jax.shard_map(
        on_device,
        mesh=mesh,
        in_specs=(
            P(None, None, None, ("track", "ses")),
            P(None, ("track", "ses")),
            P(None, ("track", "ses")),
            P(None, ("track", "ses")),
            P(None, ("track", "ses")),
            P(None, None, ("track", "ses")),
            P(("track", "ses")),
            P(None, ("track", "ses")),
            P(None, ("track", "ses")),
            P(("track", "ses"), None),
        ),
        out_specs=(P(None, ("track", "ses")), P(None, ("track", "ses")), P(None, ("track", "ses"))),
        check_vma=False,
    )
```

profile of v0, /device:TPU:1, one launch (start us, length us, event | category | flops | bytes accessed | tf_op | source)
XLA Modules:
  0.0 424.8 jit_solution(3160155488448573106)
XLA Ops:
  0.6 1.5 copy.115
  2.3 0.7 copy-done.7
  3.0 27.7 %gather_fusion = f32[8192,6]{1,0:T(8,128)} fusion(f32[6,4096]{0,1:T(8,128)S(1)} %copy.115, s32[8192]{0:T(1024)S(1)} %broadcast_clamp_fusion), kind=kCustom, calls=%fused_computation | custom fusion | bytes 425984 | tf_op jit(solution)/shard_map/gather | solution.py:61
  30.7 5.9 %copy.105 = f32[6,64,8,16]{3,2,0,1:T(8,128)} copy(f32[6,64,8,16]{0,3,2,1:T(8,128)} %bitcast.61) | data formatting | bytes 393216 | tf_op jit(solution)/shard_map/reshape | solution.py:61
  36.6 2.7 reshape.516
  39.3 14.8 %all-to-all-start = ((f32[64,1,768]{2,1,0:T(1,128)}), f32[64,1,768]{2,1,0:T(1,128)S(1)}, u32[]{:S(2)}, u32[]{:S(2)}) async-start(f32[64,1,768]{2,1,0:T(1,128)} %reshape.516), calls=%async_computation | async-start | bytes 393216 | tf_op jit(solution)/shard_map/all_to_all | solution.py:63
  54.2 11.9 %all-to-all-done = f32[64,1,768]{2,1,0:T(1,128)S(1)} async-done(((f32[64,1,768]{2,1,0:T(1,128)}), f32[64,1,768]{2,1,0:T(1,128)S(1)}, u32[]{:S(2)}, u32[]{:S(2)}) %all-to-all-start) | async-done | bytes 196640 | tf_op jit(solution)/shard_map/all_to_all | solution.py:63
  66.1 0.5 broadcast.66
  66.7 1.1 reduce
  67.8 0.5 reshape.517
  68.3 0.6 copy.106
  68.9 0.9 reshape.518
  69.8 6.8 %all-to-all-start.1 = ((f32[8,1,6144]{2,1,0:T(1,128)}), f32[8,1,6144]{2,1,0:T(1,128)S(1)}, u32[]{:S(2)}, u32[]{:S(2)}) async-start(f32[8,1,6144]{2,1,0:T(1,128)} %reshape.518), calls=%async_computation.1 | async-start | bytes 393216 | tf_op jit(solution)/shard_map/all_to_all | solution.py:62
  76.7 9.4 %all-to-all-done.1 = f32[8,1,6144]{2,1,0:T(1,128)S(1)} async-done(((f32[8,1,6144]{2,1,0:T(1,128)}), f32[8,1,6144]{2,1,0:T(1,128)S(1)}, u32[]{:S(2)}, u32[]{:S(2)}) %all-to-all-start.1) | async-done | bytes 196640 | tf_op jit(solution)/shard_map/all_to_all | solution.py:62
  86.1 1.1 reduce.1
  87.4 4.6 %copy.107 = f32[6,64,8,16]{0,3,2,1:T(8,128)} copy(f32[6,64,8,16]{1,3,0,2:T(8,128)S(1)} %bitcast.62) | data formatting | bytes 393216 | tf_op jit(solution)/shard_map/all_to_all | solution.py:62
  91.9 7.6 %gather_fusion.1 = f32[2048,6]{1,0:T(8,128)S(1)} fusion(f32[6,8192]{0,1:T(8,128)} %bitcast.60, s32[2048]{0:T(1024)S(1)} %broadcast_clamp_fusion.1), kind=kCustom, calls=%fused_computation.1 | custom fusion | bytes 106496 | tf_op jit(solution)/shard_map/gather | solution.py:70
  100.6 13.6 %scatter_custom_fusion = f32[6,8192]{0,1:T(8,128)} fusion(s32[2048]{0:T(1024)S(1)} %bitcast.74, f32[2048,6]{1,0:T(8,128)S(1)} %bitcast.68, f32[]{:T(128)} %constant.4.clone.1), kind=kCustom, calls=%fused_computation.7 | custom fusion | flops 12288 | bytes 196612 | tf_op jit(solution)/shard_map/scatter-add | solution.py:76
  114.2 5.1 %copy.110 = f32[6,64,8,16]{3,2,0,1:T(8,128)S(1)} copy(f32[6,64,8,16]{0,3,2,1:T(8,128)} %bitcast.55) | data formatting | bytes 393216 | tf_op jit(solution)/shard_map/reshape | solution.py:78
  119.3 0.6 reshape.520
  119.9 17.8 %all_to_all.20 = f32[64,1,768]{2,1,0:T(1,128)S(1)} all-to-all(f32[64,1,768]{2,1,0:T(1,128)S(1)} %reshape.520), channel_id=1, replica_groups=mesh['track'=64,'ses'=8] {'track'}, dimensions={0} | all-to-all | bytes 393216 | tf_op jit(solution)/shard_map/all_to_all | solution.py:80
  137.7 1.1 reduce.2
  138.8 0.5 reshape.521
  139.3 0.6 copy.111
  140.0 0.9 reshape.522
  140.9 3.4 all-to-all-start.3
  144.3 0.6 copy.113
  145.2 0.6 multiply_reduce_fusion.5
  145.9 8.4 %all-to-all-done.3 = f32[8,1,6144]{2,1,0:T(1,128)S(1)} async-done(((f32[8,1,6144]{2,1,0:T(1,128)}), f32[8,1,6144]{2,1,0:T(1,128)S(1)}, u32[]{:S(2)}, u32[]{:S(2)}) %all-to-all-start.3) | async-done | bytes 196640 | tf_op jit(solution)/shard_map/all_to_all | solution.py:79
  154.3 1.8 reduce.3
  156.1 1.1 reshape.523
  157.1 1.6 copy.112
  158.8 2.3 reshape.505
  161.1 2.6 copy.114
  163.7 45.1 %scatter_fusion = f32[6,4096]{0,1:T(8,128)S(1)} fusion(f32[6,4096]{0,1:T(8,128)S(1)} %copy.113, s32[8192]{0:T(1024)S(1)} %bitcast.70, f32[8192,6]{1,0:T(8,128)} %copy.114), kind=kCustom, calls=%fused_computation.3 | custom fusion | flops 49152 | bytes 622592 | tf_op jit(solution)/shard_map/scatter-add | solution.py:86
  208.8 2.7 multiply_reduce_fusion.1
  211.6 1.9 copy.119
  213.5 93.7 %all-reduce = (f32[]{:T(128)}, f32[]{:T(128)}) all-reduce(f32[]{:T(128)} %multiply_reduce_fusion.5, f32[]{:T(128)} %multiply_reduce_fusion.1), channel_id=1, replica_groups=mesh['track'=64,'ses'=8] {'track','ses'}, use_global_device_ids=true, to_apply=%region_2.0 | all-reduce | flops 2 | bytes 16 | tf_op jit(solution)/shard_map/psum | solution.py:89
  308.5 3.1 multiply_subtract_fusion
  311.6 2.2 copy.123
  314.1 2.0 copy.121
  316.1 2.8 multiply_reduce_fusion
  318.9 0.6 copy.117
  319.5 95.3 %psum.23 = f32[]{:T(128)} all-reduce(f32[]{:T(128)} %multiply_reduce_fusion), channel_id=1, replica_groups=mesh['track'=64,'ses'=8] {'track','ses'}, use_global_device_ids=true, to_apply=%region_15.0 | all-reduce | flops 1 | bytes 8 | tf_op jit(solution)/shard_map/psum | solution.py:95
  416.1 0.7 multiply_add_fusion
  416.8 2.0 copy.118
  418.8 3.2 add.67
  421.9 2.9 copy.122
  (56 shorter events, 1.8 us)
Async XLA Ops:
  0.6 1.6 copy-start.11
  2.2 34.4 %copy-start.1 = (f32[6,4096]{0,1:T(8,128)}, f32[6,4096]{0,1:T(8,128)S(1)}, u32[]{:S(2)}) copy-start(f32[6,4096]{0,1:T(8,128)S(1)} %copy.115) | copy-start | bytes 294916
  2.3 0.7 copy-start.7
  36.6 17.5 %copy-start.12 = (s32[8,256]{1,0:T(8,128)S(1)}, s32[8,256]{1,0:T(8,128)}, u32[]{:S(2)}) copy-start(s32[8,256]{1,0:T(8,128)} %param.17) | copy-start | bytes 24580
  36.6 17.6 %copy-start.13 = (s32[8,256]{1,0:T(8,128)S(1)}, s32[8,256]{1,0:T(8,128)}, u32[]{:S(2)}) copy-start(s32[8,256]{1,0:T(8,128)} %param.18) | copy-start | bytes 24580
  39.3 26.9 %all-to-all-start = ((f32[64,1,768]{2,1,0:T(1,128)}), f32[64,1,768]{2,1,0:T(1,128)S(1)}, u32[]{:S(2)}, u32[]{:S(2)}) async-start(f32[64,1,768]{2,1,0:T(1,128)} %reshape.516), calls=%async_computation | async-start | bytes 393216 | tf_op jit(solution)/shard_map/all_to_all | solution.py:63
  69.8 16.3 %all-to-all-start.1 = ((f32[8,1,6144]{2,1,0:T(1,128)}), f32[8,1,6144]{2,1,0:T(1,128)S(1)}, u32[]{:S(2)}, u32[]{:S(2)}) async-start(f32[8,1,6144]{2,1,0:T(1,128)} %reshape.518), calls=%async_computation.1 | async-start | bytes 393216 | tf_op jit(solution)/shard_map/all_to_all | solution.py:62
  87.4 12.6 %copy-start.5 = (f32[2,9,8,256]{3,2,1,0:T(8,128)S(1)}, f32[2,9,8,256]{3,2,1,0:T(8,128)}, u32[]{:S(2)}) copy-start(f32[2,9,8,256]{3,2,1,0:T(8,128)} %param.10) | copy-start | bytes 442372
  87.4 12.7 %copy-start.14 = (f32[256]{0:T(256)S(1)}, f32[256]{0:T(256)}, u32[]{:S(2)}) copy-start(f32[256]{0:T(256)} %param.16) | copy-start | bytes 3076
  138.8 5.5 %copy-start.3 = (f32[6,4096]{1,0:T(8,128)S(1)}, f32[6,4096]{1,0:T(8,128)}, u32[]{:S(2)}) copy-start(f32[6,4096]{1,0:T(8,128)} %param.11) | copy-start | bytes 294916
  138.8 5.5 %copy-start.9 = (f32[6,4096]{1,0:T(8,128)S(1)}, f32[6,4096]{1,0:T(8,128)}, u32[]{:S(2)}) copy-start(f32[6,4096]{1,0:T(8,128)} %param.14) | copy-start | bytes 294916
  140.0 5.0 %copy-start.2 = (f32[6,6,4096]{2,1,0:T(8,128)S(1)}, f32[6,6,4096]{2,1,0:T(8,128)}, u32[]{:S(2)}) copy-start(f32[6,6,4096]{2,1,0:T(8,128)} %param.15) | copy-start | bytes 1769476
  140.0 5.0 %copy-start.4 = (f32[6,4096]{1,0:T(8,128)S(1)}, f32[6,4096]{1,0:T(8,128)}, u32[]{:S(2)}) copy-start(f32[6,4096]{1,0:T(8,128)} %param.12) | copy-start | bytes 294916
  140.9 13.4 %all-to-all-start.3 = ((f32[8,1,6144]{2,1,0:T(1,128)}), f32[8,1,6144]{2,1,0:T(1,128)S(1)}, u32[]{:S(2)}, u32[]{:S(2)}) async-start(f32[8,1,6144]{2,1,0:T(1,128)} %reshape.522), calls=%async_computation.3 | async-start | bytes 393216 | tf_op jit(solution)/shard_map/all_to_all | solution.py:79
  161.1 2.6 copy-start.8
  313.8 5.0 %copy-start.6 = (f32[6,4096]{1,0:T(8,128)}, f32[6,4096]{1,0:T(8,128)S(1)}, u32[]{:S(2)}) copy-start(f32[6,4096]{1,0:T(8,128)S(1)} %copy.123) | copy-start | bytes 294916
  313.8 2.3 copy-start
  316.1 2.8 copy-start.10
where the time goes:
time: 426 us; the launch traced here: 425 us
  blocking collectives  207 us (49%)
  local copies, waits for them, and re-layouts  81.8 us (19%)
  other arithmetic  77.7 us (18%)
  waiting for transfers between devices  29.8 us (7%)
  starting transfers between devices  25 us (6%)
    psum x1, blocking collectives, on_device(): new_norm = lax.psum(jnp.sum(residual_new * precond_res), ('track', 'ses'))  95.3 us
    psum x1, blocking collectives, on_device(): old_norm = lax.psum(jnp.sum(residual * precond_old), ('track', 'ses'))  93.7 us
    scatter-add x1, other arithmetic, on_device(): jnp.zeros(direction.shape, jnp.float32).at[:, served]  45.1 us
    gather x1, local copies, waits for them, and re-layouts, on_device(): outgoing = direction[:, served].reshape(6, track_count, ses_count, capacity)  27.7 us
    all_to_all x1, blocking collectives, on_device(): lax.all_to_all(slot_sums, 'track', split_axis=1, concat_axis=1, tiled=True)  17.8 us
    unnamed x45, local copies, waits for them, and re-layouts  17.3 us
    all_to_all x1, starting transfers between devices, on_device(): lax.all_to_all(outgoing, 'track', split_axis=1, concat_axis=1, tiled=True)  14.8 us
    scatter-add x1, other arithmetic, on_device(): slot_sums = jnp.zeros(incoming.shape, jnp.float32).at[:, obs_slot.reshape...  13.6 us
  transfers between devices with their start and end apart: 3, of which 3 were waited for; matrix products, arithmetic and copies ran while one was open for 0% of the time, Pallas kernels for 0%

commit v1 on v0

v1 whole, which is shorter than its diff:
```python
import functools

import jax
import jax.numpy as jnp
from jax import lax
from jax.experimental import pallas as pl
from jax.experimental.pallas import tpu as pltpu
from jax.sharding import PartitionSpec as P

MESH = pl.DeviceIdType.MESH
VMEM = pl.BlockSpec(memory_space=pltpu.VMEM)
LANES = 256
SLOT = 8


def pieces(x):
    high = x.astype(jnp.bfloat16)
    low = (x - high.astype(jnp.float32)).astype(jnp.bfloat16)
    return jnp.concatenate([high, low], axis=0)


def join(x):
    half = x.shape[0] // 2
    return x[:half] + x[half:]


def one_hot(index, size):
    rows = lax.broadcasted_iota(jnp.int32, (size, index.shape[1]), 0)
    return jnp.where(rows == index, 1.0, 0.0).astype(jnp.bfloat16)


def pick(values, group):
    total = jnp.zeros((SLOT, values.shape[1]), jnp.float32)
    for g in range(values.shape[0] // SLOT):
        total += jnp.where(group == g, values[g * SLOT : (g + 1) * SLOT], 0.0)
    return total


def spread(values, group, groups):
    return jnp.concatenate([jnp.where(group == g, values, 0.0) for g in range(groups)], axis=0)


def dot(a, b):
    return lax.dot_general(a, b, (((1,), (0,)), ((), ())), preferred_element_type=jnp.float32)


def dot_nt(a, b):
    return lax.dot_general(a, b, (((1,), (1,)), ((), ())), preferred_element_type=jnp.float32)


def serve_kernel(direction_ref, rows_ref, out_ref, gathered):
    groups = direction_ref.shape[1] // LANES
    pad = jnp.zeros((2, LANES), jnp.float32)
    table = []
    for g in range(groups):
        table += [direction_ref[:, g * LANES : (g + 1) * LANES], pad]
    table = pieces(jnp.concatenate(table, axis=0))
    for w in range(rows_ref.shape[0]):
        index = rows_ref[w : w + 1, :]
        found = join(dot(table, one_hot(index & (LANES - 1), LANES)))
        gathered[w * SLOT : (w + 1) * SLOT, :] = pick(found, index // LANES)
    out_ref[...] = gathered[...].T


def inverse_times(m, rhs):
    a, b, c, d, e, f = m
    c00 = d * f - e * e
    c01 = e * c - b * f
    c02 = b * e - d * c
    c11 = f * a - c * c
    c12 = c * b - e * a
    c22 = a * d - b * b
    scale = 1.0 / (a * c00 + b * c01 + c * c02)
    x, y, z = rhs
    return (
        (c00 * x + c01 * y + c02 * z) * scale,
        (c01 * x + c11 * y + c12 * z) * scale,
        (c02 * x + c12 * y + c22 * z) * scale,
    )


def track_kernel(incoming_ref, jac_ref, damp_ref, slot_ref, mask_ref, out_ref, swap):
    devices = incoming_ref.shape[0]
    capacity = incoming_ref.shape[1] // SLOT
    slots, tracks = slot_ref.shape
    table = pieces(incoming_ref[...].T)
    for o in range(slots):
        slot = slot_ref[o : o + 1, :]
        found = join(dot(table, one_hot(slot // capacity, devices)))
        swap[o * SLOT : (o + 1) * SLOT, :] = pick(found, slot % capacity)
    rows = swap[...].reshape(slots, SLOT, tracks)
    camera = [rows[:, k, :] for k in range(6)]
    live = mask_ref[...].astype(jnp.float32)
    cam = [[jac_ref[a, k] for k in range(6)] for a in range(2)]
    land = [[jac_ref[a, 6 + i] for i in range(3)] for a in range(2)]
    projected = [sum(cam[a][k] * camera[k] for k in range(6)) for a in range(2)]
    weighted = [[land[a][i] * live for i in range(3)] for a in range(2)]

    def over(x):
        return jnp.sum(x, axis=0, keepdims=True)

    damp = damp_ref[...]
    normal = []
    for i in range(3):
        for j in range(i, 3):
            entry = over(sum(weighted[a][i] * land[a][j] for a in range(2)))
            normal.append(entry + damp if i == j else entry)
    rhs = [over(sum(weighted[a][i] * projected[a] for a in range(2))) for i in range(3)]
    step = inverse_times(normal, rhs)
    res = [live * (projected[a] - sum(land[a][i] * step[i] for i in range(3))) for a in range(2)]
    gradient = [sum(cam[a][k] * res[a] for a in range(2)) for k in range(6)]
    gradient += [jnp.zeros_like(live)] * 2
    rows = jnp.stack(gradient, axis=1)
    total = jnp.zeros((2 * capacity * SLOT, devices), jnp.float32)
    for o in range(slots):
        slot = slot_ref[o : o + 1, :]
        terms = pieces(spread(rows[o], slot % capacity, capacity))
        total += dot_nt(terms, one_hot(slot // capacity, devices))
    out_ref[...] = join(total).T


def apply_precond(precond, vector):
    total = precond[0] * vector[0:1]
    for k in range(1, 6):
        total += precond[k] * vector[k : k + 1]
    return total


def schur_kernel(
    arrived_ref, rows_ref, direction_ref, residual_ref, damp_ref, precond_ref,
    schur_ref, pre_res_ref, pre_schur_ref, sums_ref, turned,
):
    groups = direction_ref.shape[1] // LANES
    turned[...] = arrived_ref[...].T
    total = jnp.zeros((2 * groups * SLOT, LANES), jnp.float32)
    for w in range(rows_ref.shape[0]):
        index = rows_ref[w : w + 1, :]
        terms = pieces(spread(turned[w * SLOT : (w + 1) * SLOT, :], index // LANES, groups))
        total += dot_nt(terms, one_hot(index & (LANES - 1), LANES))
    total = join(total)
    sums = [jnp.zeros((6, LANES), jnp.float32) for _ in range(4)]
    for g in range(groups):
        part = pl.ds(g * LANES, LANES)
        direction = direction_ref[:, part]
        residual = residual_ref[:, part]
        precond = precond_ref[:, :, part]
        schur = damp_ref[:, part] * direction + total[g * SLOT : g * SLOT + 6]
        pre_res = apply_precond(precond, residual)
        pre_schur = apply_precond(precond, schur)
        schur_ref[:, part] = schur
        pre_res_ref[:, part] = pre_res
        pre_schur_ref[:, part] = pre_schur
        sums[0] += residual * pre_res
        sums[1] += direction * schur
        sums[2] += schur * pre_res
        sums[3] += schur * pre_schur
    lane = lax.broadcasted_iota(jnp.int32, (1, 128), 1)
    row = jnp.zeros((1, 128), jnp.float32)
    for q in range(4):
        row += jnp.where(lane == q, jnp.sum(sums[q], keepdims=True), 0.0)
    sums_ref[...] = row


def update_kernel(
    sums_ref, direction_ref, residual_ref, solution_ref, schur_ref, pre_res_ref, pre_schur_ref,
    solution_new_ref, residual_new_ref, direction_new_ref,
):
    old_norm, curvature, cross, square = [sums_ref[0:1, q : q + 1] for q in range(4)]
    step = old_norm / curvature
    ratio = (old_norm - 2.0 * step * cross + step * step * square) / old_norm
    direction = direction_ref[...]
    solution_new_ref[...] = solution_ref[...] + step * direction
    residual_new_ref[...] = residual_ref[...] - step * schur_ref[...]
    direction_new_ref[...] = pre_res_ref[...] - step * pre_schur_ref[...] + ratio * direction


def greet(tracks, sessions):
    me, ses = lax.axis_index("track"), lax.axis_index("ses")
    barrier = pltpu.get_barrier_semaphore()

    def track(i, _):
        pl.semaphore_signal(barrier, inc=1, device_id={"track": lax.rem(me + i, tracks)}, device_id_type=MESH)
        return 0

    lax.fori_loop(1, tracks, track, 0)
    for i in range(1, sessions):
        pl.semaphore_signal(barrier, inc=1, device_id={"ses": lax.rem(ses + i, sessions)}, device_id_type=MESH)
    pl.semaphore_wait(barrier, tracks + sessions - 2)
    return me, ses


def exchange_kernel(tracks, sessions, src, out, middle, send, recv, send2, recv2, local):
    me, ses = greet(tracks, sessions)

    def track(i, _):
        to = lax.rem(me + i, tracks)
        pltpu.make_async_remote_copy(
            src.at[to], middle.at[me], send, recv, device_id={"track": to}, device_id_type=MESH
        ).start()
        return 0

    lax.fori_loop(1, tracks, track, 0)
    own = pltpu.make_async_copy(src.at[me], middle.at[me], local.at[0])
    own.start()
    own.wait()
    others = pl.ds(0, tracks - 1)
    pltpu.make_async_copy(middle.at[others], middle.at[others], recv).wait()
    for i in range(1, sessions):
        to = lax.rem(ses + i, sessions)
        pltpu.make_async_remote_copy(
            middle.at[:, to], out.at[:, ses], send2.at[i], recv2.at[i], device_id={"ses": to}, device_id_type=MESH
        ).start()
    own = pltpu.make_async_copy(middle.at[:, ses], out.at[:, ses], local.at[1])
    own.start()
    own.wait()
    for i in range(1, sessions):
        block = out.at[:, lax.rem(ses - i + sessions, sessions)]
        pltpu.make_async_copy(block, block, recv2.at[i]).wait()
        block = middle.at[:, lax.rem(ses + i, sessions)]
        pltpu.make_async_copy(block, block, send2.at[i]).wait()
    pltpu.make_async_copy(src.at[others], src.at[others], send).wait()


def reduce_kernel(tracks, sessions, src, out, middle, final, partial, send, recv, send2, recv2, local):
    me, ses = greet(tracks, sessions)

    def track(i, _):
        to = lax.rem(me + i, tracks)
        pltpu.make_async_remote_copy(
            src, middle.at[me], send, recv, device_id={"track": to}, device_id_type=MESH
        ).start()
        return 0

    lax.fori_loop(1, tracks, track, 0)
    own = pltpu.make_async_copy(src, middle.at[me], local.at[0])
    own.start()
    own.wait()
    others = pl.ds(0, tracks - 1)
    pltpu.make_async_copy(middle.at[others], middle.at[others], recv).wait()
    partial[...] = jnp.sum(middle[...], axis=0)
    for i in range(1, sessions):
        to = lax.rem(ses + i, sessions)
        pltpu.make_async_remote_copy(
            partial, final.at[ses], send2.at[i], recv2.at[i], device_id={"ses": to}, device_id_type=MESH
        ).start()
    own = pltpu.make_async_copy(partial, final.at[ses], local.at[1])
    own.start()
    own.wait()
    for i in range(1, sessions):
        block = final.at[lax.rem(ses - i + sessions, sessions)]
        pltpu.make_async_copy(block, block, recv2.at[i]).wait()
        pltpu.make_async_copy(partial, partial, send2.at[i]).wait()
    out[...] = jnp.sum(final[...], axis=0)
    pltpu.make_async_copy(middle.at[others], middle.at[others], send).wait()


def semaphores(sessions):
    dma = pltpu.SemaphoreType.DMA
    return [dma, dma, dma((sessions,)), dma((sessions,)), dma((2,))]


def exchange(block, tracks, sessions, ident):
    shape = (tracks, sessions, 1, block.shape[-1])
    return pl.pallas_call(
        functools.partial(exchange_kernel, tracks, sessions),
        out_shape=jax.ShapeDtypeStruct(shape, jnp.float32),
        in_specs=[VMEM],
        out_specs=VMEM,
        scratch_shapes=[pltpu.VMEM(shape, jnp.float32)] + semaphores(sessions),
        compiler_params=pltpu.CompilerParams(collective_id=ident, has_side_effects=True),
        name="exchange",
    )(block.reshape(shape)).reshape(block.shape)


def reduce_all(row, tracks, sessions, ident):
    return pl.pallas_call(
        functools.partial(reduce_kernel, tracks, sessions),
        out_shape=jax.ShapeDtypeStruct(row.shape, jnp.float32),
        in_specs=[VMEM],
        out_specs=VMEM,
        scratch_shapes=[
            pltpu.VMEM((tracks,) + row.shape, jnp.float32),
            pltpu.VMEM((sessions,) + row.shape, jnp.float32),
            pltpu.VMEM(row.shape, jnp.float32),
        ]
        + semaphores(sessions),
        compiler_params=pltpu.CompilerParams(collective_id=ident, has_side_effects=True),
        name="reduce_all",
    )(row)


def local_call(kernel, outs, scratch, *args):
    return pl.pallas_call(
        kernel,
        out_shape=[jax.ShapeDtypeStruct(s, jnp.float32) for s in outs],
        in_specs=[VMEM] * len(args),
        out_specs=[VMEM] * len(outs),
        scratch_shapes=[pltpu.VMEM(s, jnp.float32) for s in scratch],
        name=kernel.__name__,
    )(*args)


def on_device(
    jacobians, direction, residual, solution, cam_damping, precond, land_damping, obs_slot, obs_mask, serve_rows
):
    tracks, sessions = lax.axis_size("track"), lax.axis_size("ses")
    devices = tracks * sessions
    capacity = serve_rows.size // devices
    rows = serve_rows.reshape(devices, capacity).T
    width = capacity * SLOT
    (outgoing,) = local_call(serve_kernel, [(devices, width)], [(width, devices)], direction, rows)
    incoming = exchange(outgoing, tracks, sessions, 0)
    (slot_sums,) = local_call(
        track_kernel,
        [(devices, width)],
        [(obs_slot.shape[0] * SLOT, obs_slot.shape[1])],
        incoming, jacobians, land_damping[None], obs_slot, obs_mask,
    )
    arrived = exchange(slot_sums, tracks, sessions, 1)
    shape = direction.shape
    schur, pre_res, pre_schur, sums = local_call(
        schur_kernel,
        [shape, shape, shape, (1, 128)],
        [(width, devices)],
        arrived, rows, direction, residual, cam_damping, precond,
    )
    sums = reduce_all(sums, tracks, sessions, 2)
    return tuple(
        local_call(update_kernel, [shape] * 3, [], sums, direction, residual, solution, schur, pre_res, pre_schur)
    )


def solution(mesh):
    split = ("track", "ses")
    return jax.shard_map(
        on_device,
        mesh=mesh,
        in_specs=(
            P(None, None, None, split),
            P(None, split),
            P(None, split),
            P(None, split),
            P(None, split),
            P(None, None, split),
            P(split),
            P(None, split),
            P(None, split),
            P(split, None),
        ),
        out_specs=(P(None, split), P(None, split), P(None, split)),
        check_vma=False,
    )
```

time: 426 us -> 97.5 us (0.23)
  blocking collectives: 207 us -> 0 us
  Pallas kernels: 0 us -> 93.6 us
  local copies, waits for them, and re-layouts: 81.8 us -> 1.35 us
  other arithmetic: 77.7 us -> 1.48 us
  waiting for transfers between devices: 29.8 us -> 0 us
  starting transfers between devices: 25 us -> 0 us
    psum x2 -> x0, blocking collectives: 189 us -> none  [the longest x1 95.3 us: on_device(): new_norm = lax.psum(jnp.sum(residual_new * precond_res), ('track', 'ses'))]
    pallas_call x0 -> x7, Pallas kernels: none -> 93.6 us  [the longest x2 62.4 us: exchange(): pl.pallas_call(functools.partial(exchange_kernel, tracks, sessions), out_...]
    scatter-add x2 -> x0, other arithmetic: 58.7 us -> none  [the longest x1 45.1 us: on_device(): jnp.zeros(direction.shape, jnp.float32).at[:, served]]
    gather x3 -> x0, local copies, waits for them, and re-layouts: 35.7 us -> none  [the longest x1 27.7 us: on_device(): outgoing = direction[:, served].reshape(6, track_count, ses_count, capacity)]
    all_to_all x3 -> x0, waiting for transfers between devices: 29.8 us -> none  [the longest x1 11.9 us: on_device(): lax.all_to_all(outgoing, 'track', split_axis=1, concat_axis=1, tiled=True)]
    all_to_all x3 -> x0, starting transfers between devices: 25 us -> none  [the longest x1 14.8 us: on_device(): lax.all_to_all(outgoing, 'track', split_axis=1, concat_axis=1, tiled=True)]
    all_to_all x1 -> x0, blocking collectives: 17.8 us -> none  [on_device(): lax.all_to_all(slot_sums, 'track', split_axis=1, concat_axis=1, tiled=True)]
    unnamed x45 -> x1, local copies, waits for them, and re-layouts: 17.3 us -> 0.51 us
  transfers between devices with their start and end apart: 3 -> 0, of which waited for: 3 -> 0; matrix products, arithmetic and copies ran while one was open for 0% -> 0% of each run, Pallas kernels for 0% -> 0%
where the time goes in v1:
time: 97.5 us; the launch traced here: 97.1 us
  Pallas kernels  93.6 us (96%)
  other arithmetic  1.48 us (2%)
  local copies, waits for them, and re-layouts  1.35 us (1%)
    pallas_call x2, Pallas kernels, exchange(): pl.pallas_call(functools.partial(exchange_kernel, tracks, sessions), out_...  62.4 us
    pallas_call x1, Pallas kernels, reduce_all(): pl.pallas_call(functools.partial(reduce_kernel, tracks, sessions), out_sh...  17.1 us
    pallas_call x4, Pallas kernels, local_call(): pl.pallas_call(kernel, out_shape=[jax.ShapeDtypeStruct(s, jnp.float32) fo...  14 us

profile of v1, /device:TPU:1, one launch (start us, length us, event | category | flops | bytes accessed | tf_op | source)
XLA Modules:
  0.0 97.1 jit_solution(9172078863879458669)
XLA Ops:
  0.6 0.5 broadcast.3
  1.1 1.5 %reduce.3 = s32[8192]{0:T(1024)S(1)} reduce(s32[1,8192]{1,0:T(1,128)} %param.19, s32[]{:T(128)} %broadcast.3), dimensions={0}, to_apply=%param.19.reduce_sub_computation.3 | reduce | bytes 65540 | tf_op args[9]
  2.6 0.1 reshape.21
  2.8 0.7 copy.13
  3.5 4.0 %serve_kernel.1 = f32[512,128]{1,0:T(8,128)} custom-call(f32[6,4096]{1,0:T(8,128)} %direction_ref.5, s32[16,512]{1,0:T(8,128)} %bitcast.10), custom_call_target="tpu_custom_call" | custom-call | tf_op jit(solution)/shard_map/serve_kernel/pallas_call | solution.py:293
  7.4 35.4 %exchange.2 = f32[64,8,1,128]{3,2,1,0:T(1,128)} custom-call(f32[64,8,1,128]{3,2,1,0:T(1,128)} %bitcast.8), custom_call_target="tpu_custom_call" | custom-call | tf_op jit(solution)/shard_map/exchange/pallas_call | solution.py:264
  42.8 3.8 %track_kernel.1 = f32[512,128]{1,0:T(8,128)} custom-call(f32[512,128]{1,0:T(8,128)} %bitcast.6, f32[2,9,8,256]{3,2,1,0:T(8,128)} %jac_ref.1, f32[1,256]{1,0:T(1,128)} %bitcast.12, s32[8,256]{1,0:T(8,128)} %slot_ref.1, s32[8,256]{1,0:T(8,128)} %mask_ref.1), custom_call_target="tpu_custom_call" | custom-call | tf_op jit(solution)/shard_map/track_kernel/pallas_call | solution.py:293
  46.6 27.1 %exchange.3 = f32[64,8,1,128]{3,2,1,0:T(1,128)} custom-call(f32[64,8,1,128]{3,2,1,0:T(1,128)} %bitcast.7), custom_call_target="tpu_custom_call" | custom-call | tf_op jit(solution)/shard_map/exchange/pallas_call | solution.py:264
  73.7 4.1 %schur_kernel.1 = (f32[6,4096]{1,0:T(8,128)}, f32[6,4096]{1,0:T(8,128)}, f32[6,4096]{1,0:T(8,128)}, f32[1,128]{1,0:T(1,128)}) custom-call(f32[512,128]{1,0:T(8,128)} %bitcast.9, s32[16,512]{1,0:T(8,128)} %bitcast.11, f32[6,4096]{1,0:T(8,128)} %direction_ref.5, f32[6,4096]{1,0:T(8,128)} %residual_ref.3, f32[6,4096]{1,0:T(8,128)} %damp_ref.1, ...), custom_call_target="tpu_custom_call" | custom-call | tf_op jit(solution)/shard_map/schur_kernel/pallas_call | solution.py:293
  77.8 17.1 %reduce_all.1.sums_ref = f32[1,128]{1,0:T(1,128)} custom-call(f32[1,128]{1,0:T(1,128)} %get-tuple-element.7.src), custom_call_target="tpu_custom_call" | custom-call | tf_op jit(solution)/shard_map/reduce_all/pallas_call | solution.py:276
  95.0 2.1 %update_kernel.1 = (f32[6,4096]{1,0:T(8,128)}, f32[6,4096]{1,0:T(8,128)}, f32[6,4096]{1,0:T(8,128)}) custom-call(f32[1,128]{1,0:T(1,128)} %reduce_all.1.sums_ref, f32[6,4096]{1,0:T(8,128)} %direction_ref.5, f32[6,4096]{1,0:T(8,128)} %residual_ref.3, f32[6,4096]{1,0:T(8,128)} %solution_ref.1, f32[6,4096]{1,0:T(8,128)} %get-tuple-element.8.schur_ref, ...), custom_call_target="tpu_custom_call" | custom-call | tf_op jit(solution)/shard_map/update_kernel/pallas_call | solution.py:293

commit v2 on v1

v2 whole, which is shorter than its diff:
```python
import functools

import jax
import jax.numpy as jnp
from jax import lax
from jax.experimental import pallas as pl
from jax.experimental.pallas import tpu as pltpu
from jax.sharding import PartitionSpec as P

MESH = pl.DeviceIdType.MESH
VMEM = pl.BlockSpec(memory_space=pltpu.VMEM)
LANES = 256
SLOT = 8


def pieces(x):
    high = x.astype(jnp.bfloat16)
    low = (x - high.astype(jnp.float32)).astype(jnp.bfloat16)
    return jnp.concatenate([high, low], axis=0)


def join(x):
    half = x.shape[0] // 2
    return x[:half] + x[half:]


def one_hot(index, size):
    rows = lax.broadcasted_iota(jnp.int32, (size, index.shape[1]), 0)
    return jnp.where(rows == index, 1.0, 0.0).astype(jnp.bfloat16)


def pick(values, group):
    total = jnp.zeros((SLOT, values.shape[1]), jnp.float32)
    for g in range(values.shape[0] // SLOT):
        total += jnp.where(group == g, values[g * SLOT : (g + 1) * SLOT], 0.0)
    return total


def spread(values, group, groups):
    return jnp.concatenate([jnp.where(group == g, values, 0.0) for g in range(groups)], axis=0)


def dot(a, b):
    return lax.dot_general(a, b, (((1,), (0,)), ((), ())), preferred_element_type=jnp.float32)


def dot_nt(a, b):
    return lax.dot_general(a, b, (((1,), (1,)), ((), ())), preferred_element_type=jnp.float32)


def turn_rows(rows_ref, tracks, sessions, capacity, index):
    width = sessions * capacity
    turned = jnp.concatenate([rows_ref[:, t * width : (t + 1) * width] for t in range(tracks)], axis=0).T
    for w in range(capacity):
        lines = [turned[y * capacity + w : y * capacity + w + 1, :] for y in range(sessions)]
        index[w : w + 1, :] = jnp.concatenate(lines, axis=1)


def serve(direction_ref, index_ref, out_ref, gathered):
    groups = direction_ref.shape[1] // LANES
    pad = jnp.zeros((2, LANES), jnp.float32)
    table = []
    for g in range(groups):
        table += [direction_ref[:, g * LANES : (g + 1) * LANES], pad]
    table = pieces(jnp.concatenate(table, axis=0))
    for w in range(index_ref.shape[0]):
        index = index_ref[w : w + 1, :]
        found = join(dot(table, one_hot(index & (LANES - 1), LANES)))
        gathered[w * SLOT : (w + 1) * SLOT, :] = pick(found, index // LANES)
    out_ref[...] = gathered[...].T.reshape(out_ref.shape)


def inverse_times(m, rhs):
    a, b, c, d, e, f = m
    c00 = d * f - e * e
    c01 = e * c - b * f
    c02 = b * e - d * c
    c11 = f * a - c * c
    c12 = c * b - e * a
    c22 = a * d - b * b
    scale = 1.0 / (a * c00 + b * c01 + c * c02)
    x, y, z = rhs
    return (
        (c00 * x + c01 * y + c02 * z) * scale,
        (c01 * x + c11 * y + c12 * z) * scale,
        (c02 * x + c12 * y + c22 * z) * scale,
    )


def track_terms(incoming_ref, jac_ref, damp_ref, slot_ref, mask_ref, out_ref, swap):
    sessions, track_count, width = incoming_ref.shape
    devices = sessions * track_count
    capacity = width // SLOT
    slots, tracks = slot_ref.shape

    def place(o):
        slot = slot_ref[o : o + 1, :]
        owner = slot // capacity
        return lax.rem(owner, sessions) * track_count + owner // sessions, slot % capacity

    table = pieces(incoming_ref[...].reshape(devices, width).T)
    for o in range(slots):
        owner, within = place(o)
        found = join(dot(table, one_hot(owner, devices)))
        swap[o * SLOT : (o + 1) * SLOT, :] = pick(found, within)
    rows = swap[...].reshape(slots, SLOT, tracks)
    camera = [rows[:, k, :] for k in range(6)]
    live = mask_ref[...].astype(jnp.float32)
    cam = [[jac_ref[a, k] for k in range(6)] for a in range(2)]
    land = [[jac_ref[a, 6 + i] for i in range(3)] for a in range(2)]
    projected = [sum(cam[a][k] * camera[k] for k in range(6)) for a in range(2)]
    weighted = [[land[a][i] * live for i in range(3)] for a in range(2)]

    def over(x):
        return jnp.sum(x, axis=0, keepdims=True)

    damp = damp_ref[...]
    normal = []
    for i in range(3):
        for j in range(i, 3):
            entry = over(sum(weighted[a][i] * land[a][j] for a in range(2)))
            normal.append(entry + damp if i == j else entry)
    rhs = [over(sum(weighted[a][i] * projected[a] for a in range(2))) for i in range(3)]
    step = inverse_times(normal, rhs)
    res = [live * (projected[a] - sum(land[a][i] * step[i] for i in range(3))) for a in range(2)]
    gradient = [sum(cam[a][k] * res[a] for a in range(2)) for k in range(6)]
    gradient += [jnp.zeros_like(live)] * 2
    rows = jnp.stack(gradient, axis=1)
    total = jnp.zeros((2 * capacity * SLOT, devices), jnp.float32)
    for o in range(slots):
        owner, within = place(o)
        terms = pieces(spread(rows[o], within, capacity))
        total += dot_nt(terms, one_hot(owner, devices))
    out_ref[...] = join(total).T.reshape(out_ref.shape)


def apply_precond(precond, vector):
    total = precond[0] * vector[0:1]
    for k in range(1, 6):
        total += precond[k] * vector[k : k + 1]
    return total


def residual_terms(residual_ref, precond_ref, pre_res_ref):
    total = jnp.zeros((6, LANES), jnp.float32)
    for g in range(residual_ref.shape[1] // LANES):
        part = pl.ds(g * LANES, LANES)
        residual = residual_ref[:, part]
        pre_res = apply_precond(precond_ref[:, :, part], residual)
        pre_res_ref[:, part] = pre_res
        total += residual * pre_res
    return total


def schur_terms(
    arrived_ref, index_ref, direction_ref, damp_ref, precond_ref, pre_res_ref, schur_ref, pre_schur_ref, turned
):
    groups = direction_ref.shape[1] // LANES
    sessions, tracks, width = arrived_ref.shape
    turned[...] = arrived_ref[...].reshape(sessions * tracks, width).T
    total = jnp.zeros((2 * groups * SLOT, LANES), jnp.float32)
    for w in range(index_ref.shape[0]):
        index = index_ref[w : w + 1, :]
        terms = pieces(spread(turned[w * SLOT : (w + 1) * SLOT, :], index // LANES, groups))
        total += dot_nt(terms, one_hot(index & (LANES - 1), LANES))
    total = join(total)
    sums = [jnp.zeros((6, LANES), jnp.float32) for _ in range(3)]
    for g in range(groups):
        part = pl.ds(g * LANES, LANES)
        direction = direction_ref[:, part]
        schur = damp_ref[:, part] * direction + total[g * SLOT : g * SLOT + 6]
        pre_schur = apply_precond(precond_ref[:, :, part], schur)
        schur_ref[:, part] = schur
        pre_schur_ref[:, part] = pre_schur
        sums[0] += direction * schur
        sums[1] += schur * pre_res_ref[:, part]
        sums[2] += schur * pre_schur
    return sums


def sums_row(sums):
    lane = lax.broadcasted_iota(jnp.int32, (1, 128), 1)
    row = jnp.zeros((1, 128), jnp.float32)
    for q in range(4):
        row += jnp.where(lane == q, jnp.sum(sums[q], keepdims=True), 0.0)
    return row


def update_kernel(
    sums_ref, direction_ref, residual_ref, solution_ref, schur_ref, pre_res_ref, pre_schur_ref,
    solution_new_ref, residual_new_ref, direction_new_ref,
):
    old_norm, curvature, cross, square = [sums_ref[0:1, q : q + 1] for q in range(4)]
    step = old_norm / curvature
    ratio = (old_norm - 2.0 * step * cross + step * step * square) / old_norm
    direction = direction_ref[...]
    solution_new_ref[...] = solution_ref[...] + step * direction
    residual_new_ref[...] = residual_ref[...] - step * schur_ref[...]
    direction_new_ref[...] = pre_res_ref[...] - step * pre_schur_ref[...] + ratio * direction


def greet(tracks, sessions):
    me, ses = lax.axis_index("track"), lax.axis_index("ses")
    barrier = pltpu.get_barrier_semaphore()

    def track(i, _):
        pl.semaphore_signal(barrier, inc=1, device_id={"track": lax.rem(me + i, tracks)}, device_id_type=MESH)
        return 0

    lax.fori_loop(1, tracks, track, 0)
    for i in range(1, sessions):
        pl.semaphore_signal(barrier, inc=1, device_id={"ses": lax.rem(ses + i, sessions)}, device_id_type=MESH)
    return me, ses, barrier


def send_tracks(me, tracks, half, size, src, middle, send, recv):
    part = pl.ds(half * size, size)

    def track(i, _):
        to = lax.rem(me + i, tracks)
        pltpu.make_async_remote_copy(
            src.at[part, to], middle.at[part, me], send, recv, device_id={"track": to}, device_id_type=MESH
        ).start()
        return 0

    lax.fori_loop(1, tracks, track, 0)


def exchange(me, ses, tracks, sessions, src, middle, out, send, recv, send2, recv2, local, between):
    size = sessions // 2
    mine = ses // size
    halves = (1 - mine, mine)
    for h in range(2):
        send_tracks(me, tracks, halves[h], size, src, middle, send.at[h], recv.at[h])
    own = pltpu.make_async_copy(src.at[:, me], middle.at[:, me], local.at[0])
    own.start()
    result = between()
    own.wait()
    others = pl.ds(0, tracks - 1)
    waits = middle.at[pl.ds(0, size), others]
    count = 0
    for h in range(2):
        pltpu.make_async_copy(waits, waits, recv.at[h]).wait()
        for i in range(size):
            offset = i if h == 0 else i + 1
            if h == 1 and i == size - 1:
                own = pltpu.make_async_copy(middle.at[ses], out.at[ses], local.at[1])
                own.start()
                continue
            to = halves[h] * size + lax.rem(ses + offset, size)
            pltpu.make_async_remote_copy(
                middle.at[to], out.at[ses], send2.at[count], recv2.at[count],
                device_id={"ses": to}, device_id_type=MESH,
            ).start()
            count += 1
    own.wait()
    for i in range(sessions - 1):
        pltpu.make_async_copy(out.at[0], out.at[0], recv2.at[i]).wait()
    return result


def exchange_end(tracks, sessions, src, middle, send, send2):
    sent = src.at[pl.ds(0, sessions // 2), pl.ds(0, tracks - 1)]
    for h in range(2):
        pltpu.make_async_copy(sent, sent, send.at[h]).wait()
    for i in range(sessions - 1):
        pltpu.make_async_copy(middle.at[0], middle.at[0], send2.at[i]).wait()


def reduce_all(me, ses, tracks, sessions, row, out, mine, middle, partial, final, send, recv, send2, recv2, local):
    mine[...] = row

    def track(i, _):
        to = lax.rem(me + i, tracks)
        pltpu.make_async_remote_copy(
            mine, middle.at[me], send, recv, device_id={"track": to}, device_id_type=MESH
        ).start()
        return 0

    lax.fori_loop(1, tracks, track, 0)
    own = pltpu.make_async_copy(mine, middle.at[me], local.at[0])
    own.start()
    own.wait()
    others = pl.ds(0, tracks - 1)
    pltpu.make_async_copy(middle.at[others], middle.at[others], recv).wait()
    partial[...] = jnp.sum(middle[...], axis=0)
    for i in range(1, sessions):
        to = lax.rem(ses + i, sessions)
        pltpu.make_async_remote_copy(
            partial, final.at[ses], send2.at[i], recv2.at[i], device_id={"ses": to}, device_id_type=MESH
        ).start()
    own = pltpu.make_async_copy(partial, final.at[ses], local.at[1])
    own.start()
    own.wait()
    for i in range(1, sessions):
        block = final.at[lax.rem(ses - i + sessions, sessions)]
        pltpu.make_async_copy(block, block, recv2.at[i]).wait()
        pltpu.make_async_copy(partial, partial, send2.at[i]).wait()
    out[...] = jnp.sum(final[...], axis=0)
    pltpu.make_async_copy(middle.at[others], middle.at[others], send).wait()


def step_kernel(
    tracks, sessions,
    jac_ref, direction_ref, residual_ref, damp_ref, precond_ref, land_ref, slot_ref, mask_ref, rows_ref,
    schur_ref, pre_res_ref, pre_schur_ref, sums_ref,
    index, turned, swap, src1, middle1, out1, src2, middle2, out2, row, middle3, partial, final,
    sems1, sems2, sems3,
):
    me, ses, barrier = greet(tracks, sessions)
    capacity = index.shape[0]
    turn_rows(rows_ref, tracks, sessions, capacity, index)
    serve(direction_ref, index, src1, turned)
    pl.semaphore_wait(barrier, tracks + sessions - 2)
    old = exchange(
        me, ses, tracks, sessions, src1, middle1, out1, *sems1,
        lambda: residual_terms(residual_ref, precond_ref, pre_res_ref),
    )
    track_terms(out1, jac_ref, land_ref, slot_ref, mask_ref, src2, swap)
    exchange(
        me, ses, tracks, sessions, src2, middle2, out2, *sems2,
        lambda: exchange_end(tracks, sessions, src1, middle1, sems1[0], sems1[2]),
    )
    rest = schur_terms(
        out2, index, direction_ref, damp_ref, precond_ref, pre_res_ref, schur_ref, pre_schur_ref, turned
    )
    reduce_all(
        me, ses, tracks, sessions, sums_row([old] + rest), sums_ref, row, middle3, partial, final, *sems3
    )
    exchange_end(tracks, sessions, src2, middle2, sems2[0], sems2[2])


def local_call(kernel, outs, scratch, *args):
    return pl.pallas_call(
        kernel,
        out_shape=[jax.ShapeDtypeStruct(s, jnp.float32) for s in outs],
        in_specs=[VMEM] * len(args),
        out_specs=[VMEM] * len(outs),
        scratch_shapes=[pltpu.VMEM(s, jnp.float32) for s in scratch],
        name=kernel.__name__,
    )(*args)


def on_device(
    jacobians, direction, residual, solution, cam_damping, precond, land_damping, obs_slot, obs_mask, serve_rows
):
    tracks, sessions = lax.axis_size("track"), lax.axis_size("ses")
    devices = tracks * sessions
    capacity = serve_rows.size // devices
    width = capacity * SLOT
    shape = direction.shape
    dma = pltpu.SemaphoreType.DMA
    block = pltpu.VMEM((sessions, tracks, width), jnp.float32)
    line = (1, 128)
    sems = [dma((2,)), dma((2,)), dma((sessions,)), dma((sessions,)), dma((2,))]
    args = (
        jacobians, direction, residual, cam_damping, precond, land_damping[None], obs_slot, obs_mask, serve_rows
    )
    schur, pre_res, pre_schur, sums = pl.pallas_call(
        functools.partial(step_kernel, tracks, sessions),
        out_shape=[jax.ShapeDtypeStruct(s, jnp.float32) for s in (shape, shape, shape, line)],
        in_specs=[VMEM] * len(args),
        out_specs=[VMEM] * 4,
        scratch_shapes=[
            pltpu.VMEM((capacity, devices), jnp.int32),
            pltpu.VMEM((width, devices), jnp.float32),
            pltpu.VMEM((obs_slot.shape[0] * SLOT, obs_slot.shape[1]), jnp.float32),
        ]
        + [block] * 6
        + [
            pltpu.VMEM(line, jnp.float32),
            pltpu.VMEM((tracks,) + line, jnp.float32),
            pltpu.VMEM(line, jnp.float32),
            pltpu.VMEM((sessions,) + line, jnp.float32),
            tuple(sems),
            tuple(sems),
            (dma, dma, dma((sessions,)), dma((sessions,)), dma((2,))),
        ],
        compiler_params=pltpu.CompilerParams(collective_id=0, has_side_effects=True),
        name="step",
    )(*args)
    return tuple(
        local_call(update_kernel, [shape] * 3, [], sums, direction, residual, solution, schur, pre_res, pre_schur)
    )


def solution(mesh):
    split = ("track", "ses")
    return jax.shard_map(
        on_device,
        mesh=mesh,
        in_specs=(
            P(None, None, None, split),
            P(None, split),
            P(None, split),
            P(None, split),
            P(None, split),
            P(None, None, split),
            P(split),
            P(None, split),
            P(None, split),
            P(split, None),
        ),
        out_specs=(P(None, split), P(None, split), P(None, split)),
        check_vma=False,
    )
```

time: 97.5 us -> 68.8 us (0.71)
  Pallas kernels: 93.6 us -> 68 us
  other arithmetic: 1.48 us -> 0 us
  local copies, waits for them, and re-layouts: 1.35 us -> 0 us
    pallas_call x3 -> x1, Pallas kernels: 79.6 us -> 65.9 us  [on_device(): pl.pallas_call(functools.partial(step_kernel, tracks, sessions), out_shap...]
    pallas_call x4 -> x1, Pallas kernels: 14 us -> 2.12 us  [local_call(): pl.pallas_call(kernel, out_shape=[jax.ShapeDtypeStruct(s, jnp.float32) fo...]
    unnamed x1 -> x0, other arithmetic: 1.48 us -> none
where the time goes in v2:
time: 68.8 us; the launch traced here: 68.7 us
  Pallas kernels  68 us (99%)
    pallas_call x1, Pallas kernels, on_device(): pl.pallas_call(functools.partial(step_kernel, tracks, sessions), out_shap...  65.9 us
    pallas_call x1, Pallas kernels, local_call(): pl.pallas_call(kernel, out_shape=[jax.ShapeDtypeStruct(s, jnp.float32) fo...  2.12 us

profile of v2, /device:TPU:1, one launch (start us, length us, event | category | flops | bytes accessed | tf_op | source)
XLA Modules:
  0.0 68.7 jit_solution(13711588347366103524)
XLA Ops:
  0.6 65.9 %step.1 = (f32[6,4096]{1,0:T(8,128)}, f32[6,4096]{1,0:T(8,128)}, f32[6,4096]{1,0:T(8,128)}, f32[1,128]{1,0:T(1,128)}) custom-call(f32[2,9,8,256]{3,2,1,0:T(8,128)} %jac_ref.1, f32[6,4096]{1,0:T(8,128)} %direction_ref.3, f32[6,4096]{1,0:T(8,128)} %residual_ref.3, f32[6,4096]{1,0:T(8,128)} %damp_ref.1, f32[6,6,4096]{2,1,0:T(8,128)} %precond_ref.1, ...), custom_call_target="tpu_custom_call" | custom-call | tf_op jit(solution)/shard_map/step/pallas_call | solution.py:359
  66.5 2.1 %update_kernel.1 = (f32[6,4096]{1,0:T(8,128)}, f32[6,4096]{1,0:T(8,128)}, f32[6,4096]{1,0:T(8,128)}) custom-call(f32[1,128]{1,0:T(1,128)} %get-tuple-element.7.sums_ref, f32[6,4096]{1,0:T(8,128)} %direction_ref.3, f32[6,4096]{1,0:T(8,128)} %residual_ref.3, f32[6,4096]{1,0:T(8,128)} %solution_ref.1, f32[6,4096]{1,0:T(8,128)} %get-tuple-element.8.schur_ref, ...), custom_call_target="tpu_custom_call" | custom-call | tf_op jit(solution)/shard_map/update_kernel/pallas_call | solution.py:334

commit v3 on v2

--- a/solution.py
+++ b/solution.py
@@ -10,6 +10,7 @@
 MESH = pl.DeviceIdType.MESH
 VMEM = pl.BlockSpec(memory_space=pltpu.VMEM)
 LANES = 256
+KEYS = 6
 SLOT = 8
 
 
@@ -38,6 +39,10 @@
 
 def spread(values, group, groups):
     return jnp.concatenate([jnp.where(group == g, values, 0.0) for g in range(groups)], axis=0)
+
+
+def slot_mask(within, capacity):
+    return lax.broadcasted_iota(jnp.int32, (capacity, within.shape[1]), 0) == within
 
 
 def dot(a, b):
@@ -56,18 +61,23 @@
         index[w : w + 1, :] = jnp.concatenate(lines, axis=1)
 
 
-def serve(direction_ref, index_ref, out_ref, gathered):
+def serve(direction_ref, index_ref, hot_ref, out_ref, tiles):
     groups = direction_ref.shape[1] // LANES
+    capacity = index_ref.shape[0]
     pad = jnp.zeros((2, LANES), jnp.float32)
     table = []
     for g in range(groups):
         table += [direction_ref[:, g * LANES : (g + 1) * LANES], pad]
     table = pieces(jnp.concatenate(table, axis=0))
-    for w in range(index_ref.shape[0]):
+    for w in range(capacity):
         index = index_ref[w : w + 1, :]
-        found = join(dot(table, one_hot(index & (LANES - 1), LANES)))
-        gathered[w * SLOT : (w + 1) * SLOT, :] = pick(found, index // LANES)
-    out_ref[...] = gathered[...].T.reshape(out_ref.shape)
+        hot = one_hot(index & (LANES - 1), LANES)
+        hot_ref[w] = hot
+        found = pick(join(dot(table, hot)), index // LANES)
+        for j in range(tiles.shape[0]):
+            tiles[j, pl.ds(w, SLOT, stride=capacity), :] = found[:, j * 128 : (j + 1) * 128]
+    turned = [tiles[j, : KEYS * capacity, :].T for j in range(tiles.shape[0])]
+    out_ref[...] = jnp.concatenate(turned, axis=0).reshape(out_ref.shape)
 
 
 def inverse_times(m, rhs):
@@ -87,24 +97,26 @@
     )
 
 
-def track_terms(incoming_ref, jac_ref, damp_ref, slot_ref, mask_ref, out_ref, swap):
+def owner_hots(slot_ref, sessions, tracks, capacity, hot_ref):
+    for o in range(slot_ref.shape[0]):
+        owner = slot_ref[o : o + 1, :] // capacity
+        place = lax.rem(owner, sessions) * tracks + owner // sessions
+        hot_ref[o] = one_hot(place, sessions * tracks)
+
+
+def track_terms(incoming_ref, jac_ref, damp_ref, slot_ref, mask_ref, hot_ref, out_ref, swap):
     sessions, track_count, width = incoming_ref.shape
     devices = sessions * track_count
-    capacity = width // SLOT
-    slots, tracks = slot_ref.shape
-
-    def place(o):
-        slot = slot_ref[o : o + 1, :]
-        owner = slot // capacity
-        return lax.rem(owner, sessions) * track_count + owner // sessions, slot % capacity
-
+    capacity = width // KEYS
+    slots = slot_ref.shape[0]
     table = pieces(incoming_ref[...].reshape(devices, width).T)
+    masks = [slot_mask(slot_ref[o : o + 1, :] % capacity, capacity) for o in range(slots)]
     for o in range(slots):
-        owner, within = place(o)
-        found = join(dot(table, one_hot(owner, devices)))
-        swap[o * SLOT : (o + 1) * SLOT, :] = pick(found, within)
-    rows = swap[...].reshape(slots, SLOT, tracks)
-    camera = [rows[:, k, :] for k in range(6)]
+        found = join(dot(table, hot_ref[o]))
+        for k in range(KEYS):
+            chosen = jnp.where(masks[o], found[k * capacity : (k + 1) * capacity], 0.0)
+            swap[k * slots + o : k * slots + o + 1, :] = jnp.sum(chosen, axis=0, keepdims=True)
+    camera = [swap[k * slots : (k + 1) * slots, :] for k in range(KEYS)]
     live = mask_ref[...].astype(jnp.float32)
     cam = [[jac_ref[a, k] for k in range(6)] for a in range(2)]
     land = [[jac_ref[a, 6 + i] for i in range(3)] for a in range(2)]
@@ -124,13 +136,10 @@
     step = inverse_times(normal, rhs)
     res = [live * (projected[a] - sum(land[a][i] * step[i] for i in range(3))) for a in range(2)]
     gradient = [sum(cam[a][k] * res[a] for a in range(2)) for k in range(6)]
-    gradient += [jnp.zeros_like(live)] * 2
-    rows = jnp.stack(gradient, axis=1)
-    total = jnp.zeros((2 * capacity * SLOT, devices), jnp.float32)
+    total = jnp.zeros((2 * width, devices), jnp.float32)
     for o in range(slots):
-        owner, within = place(o)
-        terms = pieces(spread(rows[o], within, capacity))
-        total += dot_nt(terms, one_hot(owner, devices))
+        terms = [jnp.where(masks[o], gradient[k][o : o + 1], 0.0) for k in range(KEYS)]
+        total += dot_nt(pieces(jnp.concatenate(terms, axis=0)), hot_ref[o])
     out_ref[...] = join(total).T.reshape(out_ref.shape)
 
 
@@ -153,16 +162,21 @@
 
 
 def schur_terms(
-    arrived_ref, index_ref, direction_ref, damp_ref, precond_ref, pre_res_ref, schur_ref, pre_schur_ref, turned
+    arrived_ref, index_ref, hot_ref, direction_ref, damp_ref, precond_ref, pre_res_ref, schur_ref, pre_schur_ref, tiles
 ):
     groups = direction_ref.shape[1] // LANES
     sessions, tracks, width = arrived_ref.shape
-    turned[...] = arrived_ref[...].reshape(sessions * tracks, width).T
+    capacity = index_ref.shape[0]
+    turned = arrived_ref[...].reshape(sessions * tracks, width).T
+    count = tiles.shape[0]
+    for j in range(count):
+        tiles[j, :width, :] = turned[:, j * 128 : (j + 1) * 128]
     total = jnp.zeros((2 * groups * SLOT, LANES), jnp.float32)
     for w in range(index_ref.shape[0]):
         index = index_ref[w : w + 1, :]
-        terms = pieces(spread(turned[w * SLOT : (w + 1) * SLOT, :], index // LANES, groups))
-        total += dot_nt(terms, one_hot(index & (LANES - 1), LANES))
+        lines = [tiles[j, pl.ds(w, SLOT, stride=capacity), :] for j in range(count)]
+        terms = pieces(spread(jnp.concatenate(lines, axis=1), index // LANES, groups))
+        total += dot_nt(terms, hot_ref[w])
     total = join(total)
     sums = [jnp.zeros((6, LANES), jnp.float32) for _ in range(3)]
     for g in range(groups):
@@ -302,27 +316,36 @@
 
 def step_kernel(
     tracks, sessions,
-    jac_ref, direction_ref, residual_ref, damp_ref, precond_ref, land_ref, slot_ref, mask_ref, rows_ref,
+    direction_ref, rows_ref, slot_ref, mask_ref, land_ref, jac_hbm, residual_hbm, damp_hbm, precond_hbm,
     schur_ref, pre_res_ref, pre_schur_ref, sums_ref,
-    index, turned, swap, src1, middle1, out1, src2, middle2, out2, row, middle3, partial, final,
+    jac_ref, residual_ref, damp_ref, precond_ref, loads,
+    index, tiles, swap, hot, owner_hot, src1, middle1, out1, src2, middle2, out2, row, middle3, partial, final,
     sems1, sems2, sems3,
 ):
     me, ses, barrier = greet(tracks, sessions)
+    pairs = ((residual_hbm, residual_ref), (precond_hbm, precond_ref), (jac_hbm, jac_ref), (damp_hbm, damp_ref))
+    copies = [pltpu.make_async_copy(src, dst, loads.at[i]) for i, (src, dst) in enumerate(pairs)]
+    for copy in copies:
+        copy.start()
     capacity = index.shape[0]
     turn_rows(rows_ref, tracks, sessions, capacity, index)
-    serve(direction_ref, index, src1, turned)
+    serve(direction_ref, index, hot, src1, tiles)
     pl.semaphore_wait(barrier, tracks + sessions - 2)
-    old = exchange(
-        me, ses, tracks, sessions, src1, middle1, out1, *sems1,
-        lambda: residual_terms(residual_ref, precond_ref, pre_res_ref),
-    )
-    track_terms(out1, jac_ref, land_ref, slot_ref, mask_ref, src2, swap)
+
+    def during_first():
+        for copy in copies:
+            copy.wait()
+        owner_hots(slot_ref, sessions, tracks, capacity, owner_hot)
+        return residual_terms(residual_ref, precond_ref, pre_res_ref)
+
+    old = exchange(me, ses, tracks, sessions, src1, middle1, out1, *sems1, during_first)
+    track_terms(out1, jac_ref, land_ref, slot_ref, mask_ref, owner_hot, src2, swap)
     exchange(
         me, ses, tracks, sessions, src2, middle2, out2, *sems2,
         lambda: exchange_end(tracks, sessions, src1, middle1, sems1[0], sems1[2]),
     )
     rest = schur_terms(
-        out2, index, direction_ref, damp_ref, precond_ref, pre_res_ref, schur_ref, pre_schur_ref, turned
+        out2, index, hot, direction_ref, damp_ref, precond_ref, pre_res_ref, schur_ref, pre_schur_ref, tiles
     )
     reduce_all(
         me, ses, tracks, sessions, sums_row([old] + rest), sums_ref, row, middle3, partial, final, *sems3
@@ -347,24 +370,28 @@
     tracks, sessions = lax.axis_size("track"), lax.axis_size("ses")
     devices = tracks * sessions
     capacity = serve_rows.size // devices
-    width = capacity * SLOT
+    width = capacity * KEYS
+    slots, observed = obs_slot.shape
     shape = direction.shape
     dma = pltpu.SemaphoreType.DMA
     block = pltpu.VMEM((sessions, tracks, width), jnp.float32)
     line = (1, 128)
     sems = [dma((2,)), dma((2,)), dma((sessions,)), dma((sessions,)), dma((2,))]
-    args = (
-        jacobians, direction, residual, cam_damping, precond, land_damping[None], obs_slot, obs_mask, serve_rows
-    )
+    small = (direction, serve_rows, obs_slot, obs_mask, land_damping[None])
+    large = (jacobians, residual, cam_damping, precond)
     schur, pre_res, pre_schur, sums = pl.pallas_call(
         functools.partial(step_kernel, tracks, sessions),
         out_shape=[jax.ShapeDtypeStruct(s, jnp.float32) for s in (shape, shape, shape, line)],
-        in_specs=[VMEM] * len(args),
+        in_specs=[VMEM] * len(small) + [pl.BlockSpec(memory_space=pl.ANY)] * len(large),
         out_specs=[VMEM] * 4,
-        scratch_shapes=[
+        scratch_shapes=[pltpu.VMEM(x.shape, x.dtype) for x in large]
+        + [
+            dma((len(large),)),
             pltpu.VMEM((capacity, devices), jnp.int32),
-            pltpu.VMEM((width, devices), jnp.float32),
-            pltpu.VMEM((obs_slot.shape[0] * SLOT, obs_slot.shape[1]), jnp.float32),
+            pltpu.VMEM((devices // 128, capacity * SLOT, 128), jnp.float32),
+            pltpu.VMEM((slots * KEYS, observed), jnp.float32),
+            pltpu.VMEM((capacity, LANES, devices), jnp.bfloat16),
+            pltpu.VMEM((slots, devices, observed), jnp.bfloat16),
         ]
         + [block] * 6
         + [
@@ -378,7 +405,7 @@
         ],
         compiler_params=pltpu.CompilerParams(collective_id=0, has_side_effects=True),
         name="step",
-    )(*args)
+    )(*small, *large)
     return tuple(
         local_call(update_kernel, [shape] * 3, [], sums, direction, residual, solution, schur, pre_res, pre_schur)
     )

time: 68.8 us -> 68.9 us (level)
  no operation moved by 1% of the time
where the time goes in v3:
time: 68.9 us; the launch traced here: 68.7 us
  Pallas kernels  68.1 us (99%)
    pallas_call x1, Pallas kernels, on_device(): pl.pallas_call(functools.partial(step_kernel, tracks, sessions), out_shap...  65.9 us
    pallas_call x1, Pallas kernels, local_call(): pl.pallas_call(kernel, out_shape=[jax.ShapeDtypeStruct(s, jnp.float32) fo...  2.12 us

profile of v3, /device:TPU:1, one launch (start us, length us, event | category | flops | bytes accessed | tf_op | source)
XLA Modules:
  0.0 68.7 jit_solution(11641896490892334487)
XLA Ops:
  0.6 65.9 %step.1 = (f32[6,4096]{1,0:T(8,128)}, f32[6,4096]{1,0:T(8,128)}, f32[6,4096]{1,0:T(8,128)}, f32[1,128]{1,0:T(1,128)}) custom-call(f32[6,4096]{1,0:T(8,128)} %direction_ref.3, s32[1,8192]{1,0:T(1,128)} %rows_ref.1, s32[8,256]{1,0:T(8,128)} %slot_ref.1, s32[8,256]{1,0:T(8,128)} %mask_ref.1, f32[1,256]{1,0:T(1,128)} %bitcast.1, f32[2,9,8,256]{3,2,1,0:T(8,128)} %jac_hbm.1, ...), custom_call_target="tpu_custom_call" | custom-call | tf_op jit(solution)/shard_map/step/pallas_call | solution.py:382
  66.6 2.1 %update_kernel.1 = (f32[6,4096]{1,0:T(8,128)}, f32[6,4096]{1,0:T(8,128)}, f32[6,4096]{1,0:T(8,128)}) custom-call(f32[1,128]{1,0:T(1,128)} %get-tuple-element.7.sums_ref, f32[6,4096]{1,0:T(8,128)} %direction_ref.3, f32[6,4096]{1,0:T(8,128)} %residual_ref.1, f32[6,4096]{1,0:T(8,128)} %solution_ref.1, f32[6,4096]{1,0:T(8,128)} %get-tuple-element.8.schur_ref, ...), custom_call_target="tpu_custom_call" | custom-call | tf_op jit(solution)/shard_map/update_kernel/pallas_call | solution.py:357

commit v4 on v3

--- a/solution.py
+++ b/solution.py
@@ -227,49 +227,54 @@
     return me, ses, barrier
 
 
-def send_tracks(me, tracks, half, size, src, middle, send, recv):
-    part = pl.ds(half * size, size)
-
+def send_tracks(me, tracks, src, src_at, size, dst, dst_at, send, recv):
     def track(i, _):
         to = lax.rem(me + i, tracks)
         pltpu.make_async_remote_copy(
-            src.at[part, to], middle.at[part, me], send, recv, device_id={"track": to}, device_id_type=MESH
+            src.at[pl.ds(src_at, size), to], dst.at[pl.ds(dst_at, size), me], send, recv,
+            device_id={"track": to}, device_id_type=MESH,
         ).start()
         return 0
 
     lax.fori_loop(1, tracks, track, 0)
 
 
+def send_session(ses, to, src, dst, send, recv):
+    pltpu.make_async_remote_copy(src, dst, send, recv, device_id={"ses": to}, device_id_type=MESH).start()
+
+
 def exchange(me, ses, tracks, sessions, src, middle, out, send, recv, send2, recv2, local, between):
     size = sessions // 2
-    mine = ses // size
-    halves = (1 - mine, mine)
-    for h in range(2):
-        send_tracks(me, tracks, halves[h], size, src, middle, send.at[h], recv.at[h])
-    own = pltpu.make_async_copy(src.at[:, me], middle.at[:, me], local.at[0])
-    own.start()
+    mine = ses // size * size
+    other = size - mine
+    inner = lax.rem(ses, size)
+    for i in range(1, size):
+        to = mine + lax.rem(inner + i, size)
+        send_session(ses, to, src.at[to], middle.at[ses], send2.at[i], recv2.at[i])
+    send_tracks(me, tracks, src, other, size, middle, other, send.at[0], recv.at[0])
+    own = [
+        pltpu.make_async_copy(src.at[ses], middle.at[ses], local.at[0]),
+        pltpu.make_async_copy(src.at[pl.ds(other, size), me], middle.at[pl.ds(other, size), me], local.at[1]),
+    ]
+    for copy in own:
+        copy.start()
+    for copy in own:
+        copy.wait()
+    for i in range(1, size):
+        pltpu.make_async_copy(out.at[0], out.at[0], recv2.at[i]).wait()
+    send_tracks(me, tracks, middle, mine, size, out, mine, send.at[1], recv.at[1])
     result = between()
-    own.wait()
-    others = pl.ds(0, tracks - 1)
-    waits = middle.at[pl.ds(0, size), others]
-    count = 0
-    for h in range(2):
-        pltpu.make_async_copy(waits, waits, recv.at[h]).wait()
-        for i in range(size):
-            offset = i if h == 0 else i + 1
-            if h == 1 and i == size - 1:
-                own = pltpu.make_async_copy(middle.at[ses], out.at[ses], local.at[1])
-                own.start()
-                continue
-            to = halves[h] * size + lax.rem(ses + offset, size)
-            pltpu.make_async_remote_copy(
-                middle.at[to], out.at[ses], send2.at[count], recv2.at[count],
-                device_id={"ses": to}, device_id_type=MESH,
-            ).start()
-            count += 1
-    own.wait()
-    for i in range(sessions - 1):
-        pltpu.make_async_copy(out.at[0], out.at[0], recv2.at[i]).wait()
+    waits = out.at[pl.ds(0, size), pl.ds(0, tracks - 1)]
+    pltpu.make_async_copy(waits, waits, recv.at[0]).wait()
+    for i in range(size):
+        to = other + lax.rem(inner + i, size)
+        send_session(ses, to, middle.at[to], out.at[ses], send2.at[size + i], recv2.at[size + i])
+    last = pltpu.make_async_copy(middle.at[pl.ds(mine, size), me], out.at[pl.ds(mine, size), me], local.at[0])
+    last.start()
+    last.wait()
+    pltpu.make_async_copy(waits, waits, recv.at[1]).wait()
+    for i in range(size):
+        pltpu.make_async_copy(out.at[0], out.at[0], recv2.at[size + i]).wait()
     return result
 
 
@@ -277,7 +282,7 @@
     sent = src.at[pl.ds(0, sessions // 2), pl.ds(0, tracks - 1)]
     for h in range(2):
         pltpu.make_async_copy(sent, sent, send.at[h]).wait()
-    for i in range(sessions - 1):
+    for i in range(1, sessions):
         pltpu.make_async_copy(middle.at[0], middle.at[0], send2.at[i]).wait()
 
 

time: 68.9 us -> 66.1 us (0.959)
  Pallas kernels: 68.1 us -> 65.3 us
    pallas_call x1, Pallas kernels: 65.9 us -> 63.2 us  [on_device(): pl.pallas_call(functools.partial(step_kernel, tracks, sessions), out_shap...]
where the time goes in v4:
time: 66.1 us; the launch traced here: 65.9 us
  Pallas kernels  65.3 us (99%)
    pallas_call x1, Pallas kernels, on_device(): pl.pallas_call(functools.partial(step_kernel, tracks, sessions), out_shap...  63.2 us
    pallas_call x1, Pallas kernels, local_call(): pl.pallas_call(kernel, out_shape=[jax.ShapeDtypeStruct(s, jnp.float32) fo...  2.12 us

profile of v4, /device:TPU:1, one launch (start us, length us, event | category | flops | bytes accessed | tf_op | source)
XLA Modules:
  0.0 65.9 jit_solution(11778542904366012193)
XLA Ops:
  0.6 63.2 %step.1 = (f32[6,4096]{1,0:T(8,128)}, f32[6,4096]{1,0:T(8,128)}, f32[6,4096]{1,0:T(8,128)}, f32[1,128]{1,0:T(1,128)}) custom-call(f32[6,4096]{1,0:T(8,128)} %direction_ref.3, s32[1,8192]{1,0:T(1,128)} %rows_ref.1, s32[8,256]{1,0:T(8,128)} %slot_ref.1, s32[8,256]{1,0:T(8,128)} %mask_ref.1, f32[1,256]{1,0:T(1,128)} %bitcast.1, f32[2,9,8,256]{3,2,1,0:T(8,128)} %jac_hbm.1, ...), custom_call_target="tpu_custom_call" | custom-call | tf_op jit(solution)/shard_map/step/pallas_call | solution.py:387
  63.8 2.1 %update_kernel.1 = (f32[6,4096]{1,0:T(8,128)}, f32[6,4096]{1,0:T(8,128)}, f32[6,4096]{1,0:T(8,128)}) custom-call(f32[1,128]{1,0:T(1,128)} %get-tuple-element.7.sums_ref, f32[6,4096]{1,0:T(8,128)} %direction_ref.3, f32[6,4096]{1,0:T(8,128)} %residual_ref.1, f32[6,4096]{1,0:T(8,128)} %solution_ref.1, f32[6,4096]{1,0:T(8,128)} %get-tuple-element.8.schur_ref, ...), custom_call_target="tpu_custom_call" | custom-call | tf_op jit(solution)/shard_map/update_kernel/pallas_call | solution.py:362

commit v5 on v4

--- a/solution.py
+++ b/solution.py
@@ -213,15 +213,20 @@
     direction_new_ref[...] = pre_res_ref[...] - step * pre_schur_ref[...] + ratio * direction
 
 
+def far_first(me, j, tracks):
+    step = (j + 1) // 2 * (2 * lax.rem(j, 2) - 1)
+    return lax.rem(me + tracks // 2 + step, tracks)
+
+
 def greet(tracks, sessions):
     me, ses = lax.axis_index("track"), lax.axis_index("ses")
     barrier = pltpu.get_barrier_semaphore()
 
     def track(i, _):
-        pl.semaphore_signal(barrier, inc=1, device_id={"track": lax.rem(me + i, tracks)}, device_id_type=MESH)
+        pl.semaphore_signal(barrier, inc=1, device_id={"track": far_first(me, i, tracks)}, device_id_type=MESH)
         return 0
 
-    lax.fori_loop(1, tracks, track, 0)
+    lax.fori_loop(0, tracks - 1, track, 0)
     for i in range(1, sessions):
         pl.semaphore_signal(barrier, inc=1, device_id={"ses": lax.rem(ses + i, sessions)}, device_id_type=MESH)
     return me, ses, barrier
@@ -229,14 +234,14 @@
 
 def send_tracks(me, tracks, src, src_at, size, dst, dst_at, send, recv):
     def track(i, _):
-        to = lax.rem(me + i, tracks)
+        to = far_first(me, i, tracks)
         pltpu.make_async_remote_copy(
             src.at[pl.ds(src_at, size), to], dst.at[pl.ds(dst_at, size), me], send, recv,
             device_id={"track": to}, device_id_type=MESH,
         ).start()
         return 0
 
-    lax.fori_loop(1, tracks, track, 0)
+    lax.fori_loop(0, tracks - 1, track, 0)
 
 
 def send_session(ses, to, src, dst, send, recv):
@@ -290,13 +295,13 @@
     mine[...] = row
 
     def track(i, _):
-        to = lax.rem(me + i, tracks)
+        to = far_first(me, i, tracks)
         pltpu.make_async_remote_copy(
             mine, middle.at[me], send, recv, device_id={"track": to}, device_id_type=MESH
         ).start()
         return 0
 
-    lax.fori_loop(1, tracks, track, 0)
+    lax.fori_loop(0, tracks - 1, track, 0)
     own = pltpu.make_async_copy(mine, middle.at[me], local.at[0])
     own.start()
     own.wait()

time: 66.1 us -> 65.8 us (level)
  no operation moved by 1% of the time
where the time goes in v5:
time: 65.8 us; the launch traced here: 65.6 us
  Pallas kernels  65 us (99%)
    pallas_call x1, Pallas kernels, on_device(): pl.pallas_call(functools.partial(step_kernel, tracks, sessions), out_shap...  62.9 us
    pallas_call x1, Pallas kernels, local_call(): pl.pallas_call(kernel, out_shape=[jax.ShapeDtypeStruct(s, jnp.float32) fo...  2.12 us

profile of v5, /device:TPU:1, one launch (start us, length us, event | category | flops | bytes accessed | tf_op | source)
XLA Modules:
  0.0 65.6 jit_solution(9126019980789747200)
XLA Ops:
  0.6 62.9 %step.1 = (f32[6,4096]{1,0:T(8,128)}, f32[6,4096]{1,0:T(8,128)}, f32[6,4096]{1,0:T(8,128)}, f32[1,128]{1,0:T(1,128)}) custom-call(f32[6,4096]{1,0:T(8,128)} %direction_ref.3, s32[1,8192]{1,0:T(1,128)} %rows_ref.1, s32[8,256]{1,0:T(8,128)} %slot_ref.1, s32[8,256]{1,0:T(8,128)} %mask_ref.1, f32[1,256]{1,0:T(1,128)} %bitcast.1, f32[2,9,8,256]{3,2,1,0:T(8,128)} %jac_hbm.1, ...), custom_call_target="tpu_custom_call" | custom-call | tf_op jit(solution)/shard_map/step/pallas_call | solution.py:392
  63.5 2.1 %update_kernel.1 = (f32[6,4096]{1,0:T(8,128)}, f32[6,4096]{1,0:T(8,128)}, f32[6,4096]{1,0:T(8,128)}) custom-call(f32[1,128]{1,0:T(1,128)} %get-tuple-element.7.sums_ref, f32[6,4096]{1,0:T(8,128)} %direction_ref.3, f32[6,4096]{1,0:T(8,128)} %residual_ref.1, f32[6,4096]{1,0:T(8,128)} %solution_ref.1, f32[6,4096]{1,0:T(8,128)} %get-tuple-element.8.schur_ref, ...), custom_call_target="tpu_custom_call" | custom-call | tf_op jit(solution)/shard_map/update_kernel/pallas_call | solution.py:367

commit v6 on v5

--- a/solution.py
+++ b/solution.py
@@ -326,24 +326,29 @@
 
 def step_kernel(
     tracks, sessions,
-    direction_ref, rows_ref, slot_ref, mask_ref, land_ref, jac_hbm, residual_hbm, damp_hbm, precond_hbm,
+    rows_hbm, direction_hbm, slot_hbm, mask_hbm, land_hbm, residual_hbm, precond_hbm, jac_hbm, damp_hbm,
     schur_ref, pre_res_ref, pre_schur_ref, sums_ref,
-    jac_ref, residual_ref, damp_ref, precond_ref, loads,
+    rows_ref, direction_ref, slot_ref, mask_ref, land_ref, residual_ref, precond_ref, jac_ref, damp_ref, loads,
     index, tiles, swap, hot, owner_hot, src1, middle1, out1, src2, middle2, out2, row, middle3, partial, final,
     sems1, sems2, sems3,
 ):
+    sources = (rows_hbm, direction_hbm, slot_hbm, mask_hbm, land_hbm, residual_hbm, precond_hbm, jac_hbm, damp_hbm)
+    places = (rows_ref, direction_ref, slot_ref, mask_ref, land_ref, residual_ref, precond_ref, jac_ref, damp_ref)
+    copies = [pltpu.make_async_copy(a, b, loads.at[i]) for i, (a, b) in enumerate(zip(sources, places))]
+    for copy in copies[:2]:
+        copy.start()
     me, ses, barrier = greet(tracks, sessions)
-    pairs = ((residual_hbm, residual_ref), (precond_hbm, precond_ref), (jac_hbm, jac_ref), (damp_hbm, damp_ref))
-    copies = [pltpu.make_async_copy(src, dst, loads.at[i]) for i, (src, dst) in enumerate(pairs)]
-    for copy in copies:
+    for copy in copies[2:]:
         copy.start()
+    for copy in copies[:2]:
+        copy.wait()
     capacity = index.shape[0]
     turn_rows(rows_ref, tracks, sessions, capacity, index)
     serve(direction_ref, index, hot, src1, tiles)
     pl.semaphore_wait(barrier, tracks + sessions - 2)
 
     def during_first():
-        for copy in copies:
+        for copy in copies[2:]:
             copy.wait()
         owner_hots(slot_ref, sessions, tracks, capacity, owner_hot)
         return residual_terms(residual_ref, precond_ref, pre_res_ref)
@@ -387,16 +392,17 @@
     block = pltpu.VMEM((sessions, tracks, width), jnp.float32)
     line = (1, 128)
     sems = [dma((2,)), dma((2,)), dma((sessions,)), dma((sessions,)), dma((2,))]
-    small = (direction, serve_rows, obs_slot, obs_mask, land_damping[None])
-    large = (jacobians, residual, cam_damping, precond)
+    args = (
+        serve_rows, direction, obs_slot, obs_mask, land_damping[None], residual, precond, jacobians, cam_damping
+    )
     schur, pre_res, pre_schur, sums = pl.pallas_call(
         functools.partial(step_kernel, tracks, sessions),
         out_shape=[jax.ShapeDtypeStruct(s, jnp.float32) for s in (shape, shape, shape, line)],
-        in_specs=[VMEM] * len(small) + [pl.BlockSpec(memory_space=pl.ANY)] * len(large),
+        in_specs=[pl.BlockSpec(memory_space=pl.ANY)] * len(args),
         out_specs=[VMEM] * 4,
-        scratch_shapes=[pltpu.VMEM(x.shape, x.dtype) for x in large]
+        scratch_shapes=[pltpu.VMEM(x.shape, x.dtype) for x in args]
         + [
-            dma((len(large),)),
+            dma((len(args),)),
             pltpu.VMEM((capacity, devices), jnp.int32),
             pltpu.VMEM((devices // 128, capacity * SLOT, 128), jnp.float32),
             pltpu.VMEM((slots * KEYS, observed), jnp.float32),
@@ -415,7 +421,7 @@
         ],
         compiler_params=pltpu.CompilerParams(collective_id=0, has_side_effects=True),
         name="step",
-    )(*small, *large)
+    )(*args)
     return tuple(
         local_call(update_kernel, [shape] * 3, [], sums, direction, residual, solution, schur, pre_res, pre_schur)
     )

time: 65.8 us -> 65.3 us (level)
  no operation moved by 1% of the time
where the time goes in v6:
time: 65.3 us; the launch traced here: 65.2 us
  Pallas kernels  64.5 us (99%)
    pallas_call x1, Pallas kernels, on_device(): pl.pallas_call(functools.partial(step_kernel, tracks, sessions), out_shap...  62.4 us
    pallas_call x1, Pallas kernels, local_call(): pl.pallas_call(kernel, out_shape=[jax.ShapeDtypeStruct(s, jnp.float32) fo...  2.12 us

profile of v6, /device:TPU:1, one launch (start us, length us, event | category | flops | bytes accessed | tf_op | source)
XLA Modules:
  0.0 65.2 jit_solution(14408969026726253203)
XLA Ops:
  0.6 62.4 %step.1 = (f32[6,4096]{1,0:T(8,128)}, f32[6,4096]{1,0:T(8,128)}, f32[6,4096]{1,0:T(8,128)}, f32[1,128]{1,0:T(1,128)}) custom-call(s32[1,8192]{1,0:T(1,128)} %rows_hbm.1, f32[6,4096]{1,0:T(8,128)} %direction_ref.1, s32[8,256]{1,0:T(8,128)} %slot_hbm.1, s32[8,256]{1,0:T(8,128)} %mask_hbm.1, f32[1,256]{1,0:T(1,128)} %bitcast.1, f32[6,4096]{1,0:T(8,128)} %residual_ref.1, ...), custom_call_target="tpu_custom_call" | custom-call | tf_op jit(solution)/shard_map/step/pallas_call | solution.py:398
  63.0 2.1 %update_kernel.1 = (f32[6,4096]{1,0:T(8,128)}, f32[6,4096]{1,0:T(8,128)}, f32[6,4096]{1,0:T(8,128)}) custom-call(f32[1,128]{1,0:T(1,128)} %get-tuple-element.7.sums_ref, f32[6,4096]{1,0:T(8,128)} %direction_ref.1, f32[6,4096]{1,0:T(8,128)} %residual_ref.1, f32[6,4096]{1,0:T(8,128)} %solution_ref.1, f32[6,4096]{1,0:T(8,128)} %get-tuple-element.8.schur_ref, ...), custom_call_target="tpu_custom_call" | custom-call | tf_op jit(solution)/shard_map/update_kernel/pallas_call | solution.py:372
